TPU v7x, 32 devices: a whole 2x2x4 slice. The times are simulated.
32 devices in a mesh: expert: 8 (over y, x, core), dp: 4 (over z).
Axes of the slice: x: 2, y: 2, z: 4, core: 2. Of those that a mesh axis runs over, the one named last changes fastest.
Arguments:
- tokens: bfloat16 [4096, 2048], P(('expert', 'dp')), may hold values from -6 to 6
- expert_ids: int32 [4096, 4], P(('expert', 'dp')), may hold values from 0 to 15, all different within a row; in each aligned block of 128 rows (0 to 127, 128 to 255, ...) at most 96 rows name the same one
- gate_probs: float32 [4096, 4], P(('expert', 'dp')), may hold values from 0.05 to 0.5
- expert_weights: bfloat16 [2048, 3, 16, 384], P(None, None, 'expert'), may hold values from -0.125 to 0.125
- out_grad: bfloat16 [4096, 2048], P(('expert', 'dp')), may hold values from -1.5 to 1.5
Outputs:
- layer_out: bfloat16 [4096, 2048], P(('expert', 'dp'))
- token_grad: bfloat16 [4096, 2048], P(('expert', 'dp'))
- gate_grad: float32 [4096, 4], P(('expert', 'dp'))
- weight_grad: float32 [2048, 3, 16, 384], P('dp', None, 'expert')
Inputs may be any that keep to these rules, and one draw needn't show every extreme that they name: `expert_ids`: each row names 4 different experts. Among the 128 rows of one device (aligned blocks of rows), no expert is named by more than 96 rows, and in some block some expert is named by exactly 96 rows.
All inputs are finite; a program needn't handle non-finite values.
Results may differ from a plain program's by a relative error of at most 0.0085.
Values may be sent and summed in bfloat16 or wider, within the bound.
A program may use at most 128 MiB of HBM per device.

v0:
```python
import jax
import jax.numpy as jnp
from jax import lax
from jax.sharding import PartitionSpec as P

F32 = jnp.float32
BF16 = jnp.bfloat16


def dot(a, b, ca, cb):
    return lax.dot_general(a, b, (((ca,), (cb,)), ((), ())), preferred_element_type=F32)


def local(tokens, expert_ids, gate_probs, expert_weights, out_grad):
    tok_count, top_count = expert_ids.shape
    d = tokens.shape[1]
    ranks = lax.axis_size("expert")
    me = lax.axis_index("expert")
    local_experts, h = expert_weights.shape[2:]
    n = ranks * tok_count
    eh = local_experts * h
    x = lax.all_gather(tokens, "expert", axis=0, tiled=True)
    small = jnp.concatenate([expert_ids.astype(F32), gate_probs], axis=1)
    small = lax.all_gather(small, "expert", axis=0, tiled=True)
    g = lax.all_gather(out_grad, "expert", axis=0, tiled=True)
    ids = small[:, :top_count].astype(jnp.int32)
    probs = small[:, top_count:]
    mine = me * local_experts + jnp.arange(local_experts, dtype=jnp.int32)
    hit = ids[:, :, None] == mine[None, None, :]
    p = jnp.sum(jnp.where(hit, probs[:, :, None], 0.0), axis=1)
    w = expert_weights.reshape(d, 3 * eh)
    wgu = w[:, : 2 * eh]
    wd = w[:, 2 * eh :]
    a = dot(x, wgu, 1, 0)
    gate = a[:, :eh].reshape(n, local_experts, h)
    up = a[:, eh:].reshape(n, local_experts, h)
    s = jax.nn.sigmoid(gate)
    hidden = gate * s * up
    ph = (p[:, :, None] * hidden).astype(BF16).reshape(n, eh)
    lpart = dot(ph, wd, 1, 1).astype(BF16)
    layer_out = lax.psum_scatter(lpart, "expert", scatter_dimension=0, tiled=True)
    wd_grad = dot(g, ph, 0, 0).astype(BF16)
    wd_grad = lax.psum_scatter(wd_grad, "dp", scatter_dimension=0, tiled=True)
    u = dot(g, wd, 1, 0).reshape(n, local_experts, h)
    gg = jnp.sum(u * hidden, axis=-1)
    hc = p[:, :, None] * u
    gc = (hc * up * s * (1.0 + gate * (1.0 - s))).astype(BF16).reshape(n, eh)
    uc = (hc * gate * s).astype(BF16).reshape(n, eh)
    cots = jnp.concatenate([gc, uc], axis=1)
    tpart = dot(cots, wgu, 1, 1).astype(BF16)
    token_grad = lax.psum_scatter(tpart, "expert", scatter_dimension=0, tiled=True)
    ggk = jnp.sum(jnp.where(hit, gg[:, None, :], 0.0), axis=2)
    gate_grad = lax.psum_scatter(ggk, "expert", scatter_dimension=0, tiled=True)
    wgu_grad = dot(x, cots, 0, 0).astype(BF16)
    wgu_grad = lax.psum_scatter(wgu_grad, "dp", scatter_dimension=0, tiled=True)
    wg = jnp.concatenate([wgu_grad, wd_grad], axis=1)
    weight_grad = wg.astype(F32).reshape(-1, 3, local_experts, h)
    return (layer_out, token_grad, gate_grad, weight_grad)


def solution(mesh):
    tok = P(("expert", "dp"), None)
    wsp = P(None, None, "expert", None)
    return jax.shard_map(
        local,
        mesh=mesh,
        in_specs=(tok, tok, tok, wsp, tok),
        out_specs=(tok, tok, tok, P("dp", None, "expert", None)),
        check_vma=False,
    )
```

profile of v0, /device:TPU:0, one launch (start us, length us, event | category | flops | bytes accessed | tf_op | source)
XLA Modules:
  0.0 438.3 jit_solution(9271335342334902050)
XLA Ops:
  7.2 0.0 all-gather.3.cloned.1.call-start
  7.2 0.7 all-gather.3.cloned.1.call-update
  7.9 0.0 all-gather.5.cloned.1.call-start
  7.9 0.7 all-gather.5.cloned.1.call-update
  8.6 0.0 reduce-scatter.16.cloned.1.call-start
  8.7 0.0 copy-start.6
  8.7 0.0 copy-start.7
  8.7 20.9 %reshape.38 = bf16[2048,2304]{1,0:T(8,128)(2,1)} reshape(bf16[2048,3,2,384]{3,2,1,0:T(2,128)(2,1)} %param.8) | data formatting | bytes 18874368 | tf_op jit(solution)/shard_map/reshape | solution.py:31
  29.6 0.0 copy-done.6
  29.6 0.0 copy-done.7
  29.6 10.5 %all_gather.9 = f32[1024,8]{0,1:T(8,128)S(1)} all-gather(f32[128,8]{0,1:T(8,128)S(1)} %pad_maximum_fusion.4), channel_id=1, replica_groups=mesh['expert'=8,'dp'=4] {'expert'}, dimensions={0}, use_global_device_ids=true | all-gather | bytes 36864 | tf_op jit(solution)/shard_map/all_gather | solution.py:24
  40.1 9.2 %all-gather.3.cloned.1.call-done = bf16[1024,2048]{1,0:T(8,128)(2,1)} async-done(((bf16[128,2048]{1,0:T(8,128)(2,1)}), bf16[1024,2048]{1,0:T(8,128)(2,1)}) %all-gather.3.cloned.1.call-update) | async-done | bytes 4194320 | tf_op jit(solution)/shard_map/all_gather | solution.py:22
  49.4 10.0 %fusion.3 = f32[1024,1536]{1,0:T(8,128)S(1)} fusion(bf16[1024,2048]{1,0:T(8,128)(2,1)} %all-gather.3.cloned.1.call-done, bf16[2048,2304]{1,0:T(8,128)(2,1)} %reshape.38), kind=kOutput, calls=%fused_computation.4 | convolution fusion | flops 6442450944 | bytes 16777216 | tf_op jit(solution)/shard_map/dot_general | solution.py:11
  59.4 0.0 copy-start
  59.4 3.5 fusion.16
  62.9 1.6 copy-done
  64.5 2.4 copy.35
  66.9 2.5 copy.37
  69.3 2.4 copy.38
  71.7 2.4 copy.39
  74.1 13.9 %all-gather.5.cloned.1.call-done = bf16[1024,2048]{1,0:T(8,128)(2,1)} async-done(((bf16[128,2048]{1,0:T(8,128)(2,1)}), bf16[1024,2048]{1,0:T(8,128)(2,1)}) %all-gather.5.cloned.1.call-update) | async-done | bytes 4194320 | tf_op jit(solution)/shard_map/all_gather | solution.py:25
  88.0 6.3 %fusion.9 = f32[1024,768]{0,1:T(8,128)S(1)} fusion(bf16[1024,2048]{1,0:T(8,128)(2,1)} %all-gather.5.cloned.1.call-done, bf16[2048,2304]{1,0:T(8,128)(2,1)} %reshape.38), kind=kOutput, calls=%fused_computation.16 | convolution fusion | flops 3221225472 | bytes 10485760 | tf_op jit(solution)/shard_map/dot_general | solution.py:11
  94.3 2.4 copy.34
  96.7 2.4 copy.40
  99.1 4.8 %multiply_reduce_fusion = f32[1024,2]{0,1:T(2,128)S(1)} fusion(f32[1024,2,384]{2,0,1:T(8,128)} %copy.40, f32[1024,2,384]{2,0,1:T(8,128)} %copy.39, f32[1024,2,384]{2,0,1:T(8,128)} %copy.37), kind=kLoop, calls=%fused_computation.10 | loop fusion | flops 5502976 | bytes 9445376 | tf_op jit(solution)/shard_map/reduce_sum | solution.py:45
  103.9 0.1 fusion.13
  104.0 0.2 copy.33
  104.2 2.4 mul.62
  106.7 0.0 copy-start.1
  106.7 1.9 copy.47
  108.5 1.1 copy.44
  109.6 0.0 reduce-scatter.16.cloned.1.call-update
  109.6 0.2 reduce-scatter.14.cloned.1.call-start
  109.9 0.0 copy-done.1
  109.9 0.0 copy-start.8
  109.9 6.0 %multiply_convert_fusion.1 = (bf16[1024,768]{1,0:T(8,128)(2,1)}, bf16[1024,768]{1,0:T(8,128)(2,1)}, bf16[1024,768]{1,0:T(8,128)(2,1)S(1)}) fusion(f32[1024,768]{1,0:T(8,128)} %bitcast.22, f32[1024,768]{1,0:T(8,128)S(1)} %copy-done.1, f32[1024,1536]{1,0:T(8,128)} %copy-done), kind=kLoop, calls=%fused_computation.12 | loop fusion | flops 14155776 | bytes 17301504 | tf_op jit(solution)/shard_map/convert_element_type | solution.py:47
  115.9 0.0 copy-start.2
  115.9 1.1 copy-done.2
  117.1 0.0 copy-done.8
  117.1 4.8 %fusion.8 = bf16[2048,768]{0,1:T(8,128)(2,1)} fusion(bf16[1024,768]{1,0:T(8,128)(2,1)S(1)} %get-tuple-element.32, bf16[1024,2048]{1,0:T(8,128)(2,1)S(1)} %copy-done.8), kind=kOutput, calls=%fused_computation.15 | convolution fusion | flops 3222798336 | bytes 8912896 | tf_op jit(solution)/shard_map/dot_general | solution.py:11
  121.9 0.0 copy-start.4
  121.9 0.0 copy-start.5
  121.9 0.0 reduce-scatter.14.cloned.1.call-update
  121.9 0.0 reduce-scatter.12.cloned.1.call-start
  122.0 1.3 copy-done.4
  123.3 0.5 copy-done.5
  123.8 10.9 %fusion = bf16[2048,1536]{0,1:T(8,128)(2,1)} fusion(bf16[1024,2048]{1,0:T(8,128)(2,1)} %all-gather.3.cloned.1.call-done, bf16[1024,768]{1,0:T(8,128)(2,1)S(1)} %copy-done.5, bf16[1024,768]{1,0:T(8,128)(2,1)S(1)} %copy-done.4), kind=kOutput, calls=%fused_computation.1 | convolution fusion | flops 6451888128 | bytes 13631488 | tf_op jit(solution)/shard_map/dot_general | solution.py:11
  134.7 0.0 reduce-scatter.12.cloned.1.call-update
  134.7 0.0 reduce-scatter.10.cloned.1.call-start
  134.8 11.0 %fusion.5 = bf16[1024,2048]{1,0:T(8,128)(2,1)} fusion(bf16[2048,2304]{1,0:T(8,128)(2,1)} %reshape.38, bf16[1024,768]{1,0:T(8,128)(2,1)S(1)} %copy-done.5, bf16[1024,768]{1,0:T(8,128)(2,1)S(1)} %copy-done.4), kind=kOutput, calls=%fused_computation.6 | convolution fusion | flops 6450839552 | bytes 13631488 | tf_op jit(solution)/shard_map/dot_general | solution.py:11
  145.8 0.0 copy-start.3
  145.8 0.0 reduce-scatter.10.cloned.1.call-update
  145.8 0.0 reduce-scatter.8.cloned.1.call-start
  145.8 1.3 copy-done.3
  147.2 6.9 %convolution_convert_fusion.1 = bf16[1024,2048]{1,0:T(8,128)(2,1)} fusion(bf16[1024,768]{1,0:T(8,128)(2,1)S(1)} %copy-done.3, bf16[2048,2304]{1,0:T(8,128)(2,1)} %reshape.38), kind=kOutput, calls=%fused_computation.7 | convolution fusion | flops 3223322624 | bytes 8912896 | tf_op jit(solution)/shard_map/dot_general | solution.py:11
  154.1 0.0 reduce-scatter.8.cloned.1.call-update
  154.1 0.0 reduce-scatter.16.cloned.1.call-done
  154.1 1.5 copy.45
  155.6 51.5 %reduce-scatter.14.cloned.1.call-done = bf16[512,768]{0,1:T(8,128)(2,1)} async-done(((bf16[2048,768]{0,1:T(8,128)(2,1)}), bf16[512,768]{0,1:T(8,128)(2,1)}) %reduce-scatter.14.cloned.1.call-update) | async-done | bytes 786448 | tf_op jit(solution)/shard_map/reduce_scatter | solution.py:43
  207.1 113.1 %reduce-scatter.12.cloned.1.call-done = bf16[512,1536]{0,1:T(8,128)(2,1)} async-done(((bf16[2048,1536]{0,1:T(8,128)(2,1)}), bf16[512,1536]{0,1:T(8,128)(2,1)}) %reduce-scatter.12.cloned.1.call-update) | async-done | bytes 1572880 | tf_op jit(solution)/shard_map/reduce_scatter | solution.py:55
  320.1 1.8 pad_maximum_fusion.1
  321.9 4.8 %copy.43 = f32[512,3,2,384]{3,2,1,0:T(2,128)} copy(bf16[512,3,2,384]{0,3,2,1:T(8,128)(2,1)S(1)} %bitcast.23) | data formatting | bytes 7077888
  326.7 49.5 %reduce-scatter.10.cloned.1.call-done = bf16[128,2048]{1,0:T(8,128)(2,1)} async-done(((bf16[1024,2048]{1,0:T(8,128)(2,1)}), bf16[128,2048]{1,0:T(8,128)(2,1)}) %reduce-scatter.10.cloned.1.call-update) | async-done | bytes 524304 | tf_op jit(solution)/shard_map/reduce_scatter | solution.py:51
  376.2 55.3 %reduce-scatter.8.cloned.1.call-done = bf16[128,2048]{1,0:T(8,128)(2,1)} async-done(((bf16[1024,2048]{1,0:T(8,128)(2,1)}), bf16[128,2048]{1,0:T(8,128)(2,1)}) %reduce-scatter.8.cloned.1.call-update) | async-done | bytes 524304 | tf_op jit(solution)/shard_map/reduce_scatter | solution.py:41
  (4 shorter events, 0.0 us)
Async XLA Ops:
  7.2 42.2 %all-gather.3.cloned.1.call-start = ((), (), s32[]{:S(2)}) async-start(), calls=%async_computation.5 | async-start | bytes 4718592 | tf_op jit(solution)/shard_map/all_gather | solution.py:22
  7.9 80.1 %all-gather.5.cloned.1.call-start = ((), (), s32[]{:S(2)}) async-start(), calls=%async_computation.7 | async-start | bytes 4718592 | tf_op jit(solution)/shard_map/all_gather | solution.py:25
  8.6 145.5 %reduce-scatter.16.cloned.1.call-start = ((), (), s32[]{:S(2)}) async-start(), calls=%async_computation.11 | async-start | bytes 589824
  8.7 20.9 %copy-start.6 = (s32[128,4]{0,1:T(4,128)S(1)}, s32[128,4]{0,1:T(4,128)}, u32[]{:S(2)}) copy-start(s32[128,4]{0,1:T(4,128)} %param.6) | copy-start | bytes 6148
  8.7 20.9 %copy-start.7 = (f32[128,4]{0,1:T(4,128)S(1)}, f32[128,4]{0,1:T(4,128)}, u32[]{:S(2)}) copy-start(f32[128,4]{0,1:T(4,128)} %param.7) | copy-start | bytes 6148
  59.4 5.1 %copy-start = (f32[1024,1536]{1,0:T(8,128)}, f32[1024,1536]{1,0:T(8,128)S(1)}, u32[]{:S(2)}) copy-start(f32[1024,1536]{1,0:T(8,128)S(1)} %fusion.3) | copy-start | bytes 18874372
  106.7 3.2 copy-start.1
  109.6 97.4 %reduce-scatter.14.cloned.1.call-start = ((), (), s32[]{:S(2)}) async-start(), calls=%async_computation.10 | async-start | bytes 3932160 | tf_op jit(solution)/shard_map/reduce_scatter | solution.py:43
  109.9 7.2 %copy-start.8 = (bf16[1024,2048]{1,0:T(8,128)(2,1)S(1)}, bf16[1024,2048]{1,0:T(8,128)(2,1)}, u32[]{:S(2)}) copy-start(bf16[1024,2048]{1,0:T(8,128)(2,1)} %all-gather.5.cloned.1.call-done) | copy-start | bytes 12582916
  115.9 1.1 copy-start.2
  121.9 1.4 copy-start.4
  121.9 1.9 copy-start.5
  121.9 198.2 %reduce-scatter.12.cloned.1.call-start = ((), (), s32[]{:S(2)}) async-start(), calls=%async_computation.9 | async-start | bytes 7864320 | tf_op jit(solution)/shard_map/reduce_scatter | solution.py:55
  134.7 241.5 %reduce-scatter.10.cloned.1.call-start = ((), (), s32[]{:S(2)}) async-start(), calls=%async_computation.8 | async-start | bytes 4718592 | tf_op jit(solution)/shard_map/reduce_scatter | solution.py:51
  145.8 1.4 copy-start.3
  145.8 285.7 %reduce-scatter.8.cloned.1.call-start = ((), (), s32[]{:S(2)}) async-start(), calls=%async_computation.6 | async-start | bytes 4718592 | tf_op jit(solution)/shard_map/reduce_scatter | solution.py:41
Sparse Core Ops, SparseCore 0:
  9.9 39.4 all-gather.2
  51.3 36.6 all-gather.4
  109.8 34.1 reduce-scatter.15
  146.8 60.2 reduce-scatter.13
  209.3 110.7 reduce-scatter.11
  324.3 51.8 reduce-scatter.9
  380.1 51.3 reduce-scatter.7
where the time goes:
time: 439 us; the launch traced here: 438 us
  waiting for transfers between devices  294 us (67%)
  local copies, waits for them, and re-layouts  56.4 us (13%)
  matrix products  49.9 us (11%)
  between operations  14.3 us (3%)
  other arithmetic  12.8 us (3%)
  blocking collectives  10.5 us (2%)
    reduce_scatter x1, waiting for transfers between devices, local(): wgu_grad = lax.psum_scatter(wgu_grad, 'dp', scatter_dimension=0, tiled=True)  113 us
    reduce_scatter x1, waiting for transfers between devices, local(): lax.psum_scatter(lpart, 'expert', scatter_dimension=0, tiled=True)  55.3 us
    reduce_scatter x1, waiting for transfers between devices, local(): wd_grad = lax.psum_scatter(wd_grad, 'dp', scatter_dimension=0, tiled=True)  51.5 us
    dot_general x6, matrix products, dot(): lax.dot_general(a, b, (((ca,), (cb,)), ((), ())), preferred_element_type=...  49.9 us
    reduce_scatter x1, waiting for transfers between devices, local(): lax.psum_scatter(tpart, 'expert', scatter_dimension=0, tiled=True)  49.5 us
    reshape x1, local copies, waits for them, and re-layouts, local(): w = expert_weights.reshape(d, 3 * eh)  20.9 us
    unnamed x22, local copies, waits for them, and re-layouts  15.1 us
    all_gather x1, waiting for transfers between devices, local(): g = lax.all_gather(out_grad, 'expert', axis=0, tiled=True)  13.9 us
  transfers between devices with their start and end apart: 7, of which 6 were waited for; matrix products, arithmetic and copies ran while one was open for 21% of the time, Pallas kernels for 0%

commit v1 on v0

--- a/solution.py
+++ b/solution.py
@@ -21,7 +21,15 @@
     eh = local_experts * h
     x = lax.all_gather(tokens, "expert", axis=0, tiled=True)
     small = jnp.concatenate([expert_ids.astype(F32), gate_probs], axis=1)
-    small = lax.all_gather(small, "expert", axis=0, tiled=True)
+    p_count = jax.lax.axis_size("expert")
+    low = [None] * p_count
+    low[p_count - 1] = small
+    steps_seen = tuple(((c, (c + 1) % p_count) for c in range(p_count)))
+    for to_i in range(p_count - 2, -1, -1):
+        low[to_i] = jax.lax.ppermute(low[to_i + 1], axis_name="expert", perm=steps_seen)
+    carry_in = jnp.concatenate(low, axis=0)
+    block_out = (jax.lax.axis_index("expert") + 1) * small.shape[0]
+    small = jnp.roll(carry_in, block_out, axis=0)
     g = lax.all_gather(out_grad, "expert", axis=0, tiled=True)
     ids = small[:, :top_count].astype(jnp.int32)
     probs = small[:, top_count:]

time: 439 us -> 439 us (level)
  blocking collectives: 10.5 us -> 0 us
  waiting for transfers between devices: 294 us -> 302 us
    ppermute x0 -> x7, waiting for transfers between devices: none -> 23.9 us  [local(): jax.lax.ppermute(low[to_i + 1], axis_name='expert', perm=steps_seen)]
    all_gather x1 -> x0, blocking collectives: 10.5 us -> none  [local(): small = lax.all_gather(small, 'expert', axis=0, tiled=True)]
    all_gather x1, waiting for transfers between devices: 9.23 us -> 0.01 us  [local(): x = lax.all_gather(tokens, 'expert', axis=0, tiled=True)]
    all_gather x1, waiting for transfers between devices: 13.9 us -> 7.36 us  [local(): g = lax.all_gather(out_grad, 'expert', axis=0, tiled=True)]
    unnamed x22 -> x34, local copies, waits for them, and re-layouts: 15.1 us -> 15.2 us
  transfers between devices with their start and end apart: 7 -> 14, of which waited for: 6 -> 11; matrix products, arithmetic and copies ran while one was open for 21% -> 21% of each run, Pallas kernels for 0% -> 0%
where the time goes in v1:
time: 439 us; the launch traced here: 438 us
  waiting for transfers between devices  302 us (69%)
  local copies, waits for them, and re-layouts  56.5 us (13%)
  matrix products  50.1 us (11%)
  between operations  14.4 us (3%)
  other arithmetic  14.2 us (3%)
    reduce_scatter x1, waiting for transfers between devices, local(): wgu_grad = lax.psum_scatter(wgu_grad, 'dp', scatter_dimension=0, tiled=True)  113 us
    reduce_scatter x1, waiting for transfers between devices, local(): lax.psum_scatter(lpart, 'expert', scatter_dimension=0, tiled=True)  55.3 us
    reduce_scatter x1, waiting for transfers between devices, local(): wd_grad = lax.psum_scatter(wd_grad, 'dp', scatter_dimension=0, tiled=True)  51.4 us
    dot_general x6, matrix products, dot(): lax.dot_general(a, b, (((ca,), (cb,)), ((), ())), preferred_element_type=...  50.1 us
    reduce_scatter x1, waiting for transfers between devices, local(): lax.psum_scatter(tpart, 'expert', scatter_dimension=0, tiled=True)  49.5 us
    ppermute x7, waiting for transfers between devices, local(): jax.lax.ppermute(low[to_i + 1], axis_name='expert', perm=steps_seen)  23.9 us
    reshape x1, local copies, waits for them, and re-layouts, local(): w = expert_weights.reshape(d, 3 * eh)  20.8 us
    unnamed x34, local copies, waits for them, and re-layouts  15.2 us
  transfers between devices with their start and end apart: 14, of which 11 were waited for; matrix products, arithmetic and copies ran while one was open for 21% of the time, Pallas kernels for 0%

profile of v1, /device:TPU:0, one launch (start us, length us, event | category | flops | bytes accessed | tf_op | source)
XLA Modules:
  0.0 438.2 jit_solution(2509097387834566184)
XLA Ops:
  7.2 0.0 all-gather.3.cloned.1.call-start
  7.2 0.7 all-gather.3.cloned.1.call-update
  7.9 0.0 all-gather.5.cloned.1.call-start
  7.9 0.7 all-gather.5.cloned.1.call-update
  8.6 0.0 reduce-scatter.16.cloned.1.call-start
  8.7 0.7 convert_element_type.43
  9.4 0.7 pad_maximum_fusion.4
  10.1 0.5 collective-permute-start
  10.5 4.2 collective-permute-done
  14.7 0.0 collective-permute-start.1
  14.7 3.9 collective-permute-done.1
  18.6 0.0 collective-permute-start.2
  18.6 3.9 collective-permute-done.2
  22.6 0.0 collective-permute-start.3
  22.6 4.0 collective-permute-done.3
  26.6 0.0 collective-permute-start.4
  26.6 3.9 collective-permute-done.4
  30.5 3.9 collective-permute-done.5
  34.5 0.0 collective-permute-start.6
  34.5 20.8 %reshape.38 = bf16[2048,2304]{1,0:T(8,128)(2,1)} reshape(bf16[2048,3,2,384]{3,2,1,0:T(2,128)(2,1)} %param.8) | data formatting | bytes 18874368 | tf_op jit(solution)/shard_map/reshape | solution.py:39
  55.5 0.1 fusion.17
  55.6 10.3 %fusion.3 = f32[1024,1536]{1,0:T(8,128)S(1)} fusion(bf16[1024,2048]{1,0:T(8,128)(2,1)} %all-gather.3.cloned.1.call-done, bf16[2048,2304]{1,0:T(8,128)(2,1)} %reshape.38), kind=kOutput, calls=%fused_computation.4 | convolution fusion | flops 6442450944 | bytes 16777216 | tf_op jit(solution)/shard_map/dot_general | solution.py:11
  65.8 3.5 fusion.16
  69.3 1.7 copy-done
  71.0 2.4 copy.35
  73.4 2.5 copy.37
  75.9 2.4 copy.38
  78.3 2.4 copy.39
  80.6 7.4 %all-gather.5.cloned.1.call-done = bf16[1024,2048]{1,0:T(8,128)(2,1)} async-done(((bf16[128,2048]{1,0:T(8,128)(2,1)}), bf16[1024,2048]{1,0:T(8,128)(2,1)}) %all-gather.5.cloned.1.call-update) | async-done | bytes 4194320 | tf_op jit(solution)/shard_map/all_gather | solution.py:33
  88.0 6.2 %fusion.9 = f32[1024,768]{0,1:T(8,128)S(1)} fusion(bf16[1024,2048]{1,0:T(8,128)(2,1)} %all-gather.5.cloned.1.call-done, bf16[2048,2304]{1,0:T(8,128)(2,1)} %reshape.38), kind=kOutput, calls=%fused_computation.16 | convolution fusion | flops 3221225472 | bytes 10485760 | tf_op jit(solution)/shard_map/dot_general | solution.py:11
  94.2 2.4 copy.34
  96.6 2.4 copy.40
  99.0 4.8 %multiply_reduce_fusion = f32[1024,2]{0,1:T(2,128)S(1)} fusion(f32[1024,2,384]{2,0,1:T(8,128)} %copy.40, f32[1024,2,384]{2,0,1:T(8,128)} %copy.39, f32[1024,2,384]{2,0,1:T(8,128)} %copy.37), kind=kLoop, calls=%fused_computation.10 | loop fusion | flops 5502976 | bytes 9445376 | tf_op jit(solution)/shard_map/reduce_sum | solution.py:53
  103.8 0.1 fusion.13
  103.9 0.2 copy.33
  104.1 2.4 mul.66
  106.6 1.9 copy.47
  108.4 1.1 copy.44
  109.5 0.0 reduce-scatter.16.cloned.1.call-update
  109.5 0.2 reduce-scatter.14.cloned.1.call-start
  109.8 6.0 %multiply_convert_fusion.1 = (bf16[1024,768]{1,0:T(8,128)(2,1)}, bf16[1024,768]{1,0:T(8,128)(2,1)}, bf16[1024,768]{1,0:T(8,128)(2,1)S(1)}) fusion(f32[1024,768]{1,0:T(8,128)} %bitcast.22, f32[1024,768]{1,0:T(8,128)S(1)} %copy-done.1, f32[1024,1536]{1,0:T(8,128)} %copy-done), kind=kLoop, calls=%fused_computation.12 | loop fusion | flops 14155776 | bytes 17301504 | tf_op jit(solution)/shard_map/convert_element_type | solution.py:55
  115.8 1.2 copy-done.2
  117.0 4.8 %fusion.8 = bf16[2048,768]{0,1:T(8,128)(2,1)} fusion(bf16[1024,768]{1,0:T(8,128)(2,1)S(1)} %get-tuple-element.32, bf16[1024,2048]{1,0:T(8,128)(2,1)S(1)} %copy-done.7), kind=kOutput, calls=%fused_computation.15 | convolution fusion | flops 3222798336 | bytes 8912896 | tf_op jit(solution)/shard_map/dot_general | solution.py:11
  121.8 0.0 reduce-scatter.14.cloned.1.call-update
  121.8 0.0 reduce-scatter.12.cloned.1.call-start
  121.9 1.3 copy-done.4
  123.2 0.5 copy-done.5
  123.7 10.9 %fusion = bf16[2048,1536]{0,1:T(8,128)(2,1)} fusion(bf16[1024,2048]{1,0:T(8,128)(2,1)} %all-gather.3.cloned.1.call-done, bf16[1024,768]{1,0:T(8,128)(2,1)S(1)} %copy-done.5, bf16[1024,768]{1,0:T(8,128)(2,1)S(1)} %copy-done.4), kind=kOutput, calls=%fused_computation.1 | convolution fusion | flops 6451888128 | bytes 13631488 | tf_op jit(solution)/shard_map/dot_general | solution.py:11
  134.6 0.0 reduce-scatter.12.cloned.1.call-update
  134.6 0.0 reduce-scatter.10.cloned.1.call-start
  134.7 11.0 %fusion.5 = bf16[1024,2048]{1,0:T(8,128)(2,1)} fusion(bf16[2048,2304]{1,0:T(8,128)(2,1)} %reshape.38, bf16[1024,768]{1,0:T(8,128)(2,1)S(1)} %copy-done.5, bf16[1024,768]{1,0:T(8,128)(2,1)S(1)} %copy-done.4), kind=kOutput, calls=%fused_computation.6 | convolution fusion | flops 6450839552 | bytes 13631488 | tf_op jit(solution)/shard_map/dot_general | solution.py:11
  145.7 0.0 reduce-scatter.10.cloned.1.call-update
  145.7 0.0 reduce-scatter.8.cloned.1.call-start
  145.7 1.3 copy-done.3
  147.1 6.9 %convolution_convert_fusion.1 = bf16[1024,2048]{1,0:T(8,128)(2,1)} fusion(bf16[1024,768]{1,0:T(8,128)(2,1)S(1)} %copy-done.3, bf16[2048,2304]{1,0:T(8,128)(2,1)} %reshape.38), kind=kOutput, calls=%fused_computation.7 | convolution fusion | flops 3223322624 | bytes 8912896 | tf_op jit(solution)/shard_map/dot_general | solution.py:11
  154.0 0.0 reduce-scatter.8.cloned.1.call-update
  154.0 0.0 reduce-scatter.16.cloned.1.call-done
  154.0 1.5 copy.45
  155.5 51.4 %reduce-scatter.14.cloned.1.call-done = bf16[512,768]{0,1:T(8,128)(2,1)} async-done(((bf16[2048,768]{0,1:T(8,128)(2,1)}), bf16[512,768]{0,1:T(8,128)(2,1)}) %reduce-scatter.14.cloned.1.call-update) | async-done | bytes 786448 | tf_op jit(solution)/shard_map/reduce_scatter | solution.py:51
  207.0 113.1 %reduce-scatter.12.cloned.1.call-done = bf16[512,1536]{0,1:T(8,128)(2,1)} async-done(((bf16[2048,1536]{0,1:T(8,128)(2,1)}), bf16[512,1536]{0,1:T(8,128)(2,1)}) %reduce-scatter.12.cloned.1.call-update) | async-done | bytes 1572880 | tf_op jit(solution)/shard_map/reduce_scatter | solution.py:63
  320.0 1.8 pad_maximum_fusion.1
  321.8 4.8 %copy.43 = f32[512,3,2,384]{3,2,1,0:T(2,128)} copy(bf16[512,3,2,384]{0,3,2,1:T(8,128)(2,1)S(1)} %bitcast.23) | data formatting | bytes 7077888
  326.6 49.5 %reduce-scatter.10.cloned.1.call-done = bf16[128,2048]{1,0:T(8,128)(2,1)} async-done(((bf16[1024,2048]{1,0:T(8,128)(2,1)}), bf16[128,2048]{1,0:T(8,128)(2,1)}) %reduce-scatter.10.cloned.1.call-update) | async-done | bytes 524304 | tf_op jit(solution)/shard_map/reduce_scatter | solution.py:59
  376.1 55.3 %reduce-scatter.8.cloned.1.call-done = bf16[128,2048]{1,0:T(8,128)(2,1)} async-done(((bf16[1024,2048]{1,0:T(8,128)(2,1)}), bf16[128,2048]{1,0:T(8,128)(2,1)}) %reduce-scatter.8.cloned.1.call-update) | async-done | bytes 524304 | tf_op jit(solution)/shard_map/reduce_scatter | solution.py:49
  (31 shorter events, 0.1 us)
Async XLA Ops:
  7.2 48.4 %all-gather.3.cloned.1.call-start = ((), (), s32[]{:S(2)}) async-start(), calls=%async_computation.5 | async-start | bytes 4718592 | tf_op jit(solution)/shard_map/all_gather | solution.py:22
  7.9 80.1 %all-gather.5.cloned.1.call-start = ((), (), s32[]{:S(2)}) async-start(), calls=%async_computation.7 | async-start | bytes 4718592 | tf_op jit(solution)/shard_map/all_gather | solution.py:33
  8.6 145.4 %reduce-scatter.16.cloned.1.call-start = ((), (), s32[]{:S(2)}) async-start(), calls=%async_computation.11 | async-start | bytes 589824
  10.1 4.6 %collective-permute-start = (f32[128,8]{0,1:T(8,128)S(1)}, f32[128,8]{0,1:T(8,128)S(1)}, u32[]{:S(2)}, u32[]{:S(2)}) collective-permute-start(f32[128,8]{0,1:T(8,128)S(1)} %pad_maximum_fusion.4), channel_id=1, source_target_pairs={{0,4},{4,8},{8,12},{12,16},{16,20},{20,24},{24,28},{28,0},{1,5},{5... | collective-permute-start | bytes 12296 | tf_op jit(solution)/shard_map/ppermute | solution.py:29
  14.7 3.9 collective-permute-start.1
  18.6 3.9 collective-permute-start.2
  22.6 4.0 collective-permute-start.3
  26.6 3.9 collective-permute-start.4
  30.5 3.9 collective-permute-start.5
  34.5 20.8 %collective-permute-start.6 = (f32[128,8]{0,1:T(8,128)S(1)}, f32[128,8]{0,1:T(8,128)S(1)}, u32[]{:S(2)}, u32[]{:S(2)}) collective-permute-start(f32[128,8]{0,1:T(8,128)S(1)} %collective-permute-done.5), channel_id=1, source_target_pairs={{0,4},{4,8},{8,12},{12,16},{16,20},{20,24},{24,28},{28,0},{1,5},{5... | collective-permute-start | bytes 12296 | tf_op jit(solution)/shard_map/ppermute | solution.py:29
  34.5 20.9 %copy-start.6 = (f32[128,4]{0,1:T(4,128)S(1)}, f32[128,4]{0,1:T(4,128)}, u32[]{:S(2)}) copy-start(f32[128,4]{0,1:T(4,128)} %param.7) | copy-start | bytes 6148
  65.8 5.2 %copy-start = (f32[1024,1536]{1,0:T(8,128)}, f32[1024,1536]{1,0:T(8,128)S(1)}, u32[]{:S(2)}) copy-start(f32[1024,1536]{1,0:T(8,128)S(1)} %fusion.3) | copy-start | bytes 18874372
  106.6 3.2 copy-start.1
  109.5 97.4 %reduce-scatter.14.cloned.1.call-start = ((), (), s32[]{:S(2)}) async-start(), calls=%async_computation.10 | async-start | bytes 3932160 | tf_op jit(solution)/shard_map/reduce_scatter | solution.py:51
  109.8 7.2 %copy-start.7 = (bf16[1024,2048]{1,0:T(8,128)(2,1)S(1)}, bf16[1024,2048]{1,0:T(8,128)(2,1)}, u32[]{:S(2)}) copy-start(bf16[1024,2048]{1,0:T(8,128)(2,1)} %all-gather.5.cloned.1.call-done) | copy-start | bytes 12582916
  115.8 1.2 copy-start.2
  121.8 1.4 copy-start.4
  121.8 1.9 copy-start.5
  121.8 198.2 %reduce-scatter.12.cloned.1.call-start = ((), (), s32[]{:S(2)}) async-start(), calls=%async_computation.9 | async-start | bytes 7864320 | tf_op jit(solution)/shard_map/reduce_scatter | solution.py:63
  134.6 241.5 %reduce-scatter.10.cloned.1.call-start = ((), (), s32[]{:S(2)}) async-start(), calls=%async_computation.8 | async-start | bytes 4718592 | tf_op jit(solution)/shard_map/reduce_scatter | solution.py:59
  145.7 1.4 copy-start.3
  145.7 285.6 %reduce-scatter.8.cloned.1.call-start = ((), (), s32[]{:S(2)}) async-start(), calls=%async_computation.6 | async-start | bytes 4718592 | tf_op jit(solution)/shard_map/reduce_scatter | solution.py:49
Sparse Core Ops, SparseCore 0:
  9.9 39.4 all-gather.2
  51.3 36.6 all-gather.4
  109.7 34.1 reduce-scatter.15
  146.7 60.2 reduce-scatter.13
  209.2 110.7 reduce-scatter.11
  324.2 51.8 reduce-scatter.9
  380.0 51.2 reduce-scatter.7
